TPU v7x, 32 devices: a whole 2x2x4 slice. The times are simulated.
32 devices in a mesh: expert: 4 (over z), fsdp: 8 (over y, x, core).
Axes of the slice: x: 2, y: 2, z: 4, core: 2. Of those that a mesh axis runs over, the one named last changes fastest.
Arguments:
- tokens: bfloat16 [25216, 512], P(('expert', 'fsdp')), may hold values from -6 to 6
- routes: int32 [25216, 2], P(('expert', 'fsdp')), may hold values from 0 to 7, all different within a row; in each aligned block of 788 rows (0 to 787, 788 to 1575, ...) at most 394 rows name the same one
- cotangent: bfloat16 [25216, 512], P(('expert', 'fsdp')), may hold values from -6 to 6
- attend_gain: float32 [512], P('fsdp'), may hold values from 0.5 to 1.5
- attend_bias: float32 [512], P('fsdp'), may hold values from -1.25 to 1.25
- triple_weight: float32 [512, 1536], P('fsdp'), may hold values from -0.25 to 0.25
- merge_weight: float32 [512, 512], P('fsdp'), may hold values from -2 to 2
- mixture_gain: float32 [512], P('fsdp'), may hold values from 0.5 to 1.5
- mixture_bias: float32 [512], P('fsdp'), may hold values from -1.25 to 1.25
- router_weight: float32 [512, 8], P('fsdp'), may hold values from -0.125 to 0.125
- expert_up: float32 [8, 512, 2048], P('expert', 'fsdp'), may hold values from -0.25 to 0.25
- expert_down: float32 [8, 2048, 512], P('expert', 'fsdp'), may hold values from -0.75 to 0.75
Outputs:
- block_out: bfloat16 [25216, 512], P(('expert', 'fsdp'))
- tokens_grad: float32 [25216, 512], P(('expert', 'fsdp'))
- attendgain_grad: float32 [512], P('fsdp')
- attendbias_grad: float32 [512], P('fsdp')
- triple_grad: float32 [512, 1536], P('fsdp')
- merge_grad: float32 [512, 512], P('fsdp')
- mixturegain_grad: float32 [512], P('fsdp')
- mixturebias_grad: float32 [512], P('fsdp')
- router_grad: float32 [512, 8], P('fsdp')
- expertup_grad: float32 [8, 512, 2048], P('expert', 'fsdp')
- expertdown_grad: float32 [8, 2048, 512], P('expert', 'fsdp')
Inputs may be any that keep to these rules, and one draw needn't show every extreme that they name: `routes`: each token names 2 different experts. Among the 788 tokens of one device no expert is named by more than 394 tokens, a bound that some block reaches of them; every expert is named by some token.
All inputs are finite; a program needn't handle non-finite values.
Results may differ from a plain program's by a relative error of at most 0.02.
Values may be sent and summed in bfloat16 or wider, within the bound.
A program may use at most 192 MiB of HBM per device.

v0:
```python
from functools import partial
import jax
import jax.numpy as jnp
from jax import lax
from jax.sharding import PartitionSpec as P

HEAD_DIM = 64
TOP = 2
SEQ = 197
EPSILON = 1e-06


def layer_norm(values, gain, bias):
    center = values - jnp.mean(values, -1, keepdims=True)
    spread = jnp.mean(center * center, -1, keepdims=True)
    return center * lax.rsqrt(spread + EPSILON) * gain + bias


def local(
    tokens,
    routes,
    cotangent,
    attend_gain,
    attend_bias,
    triple_weight,
    merge_weight,
    mixture_gain,
    mixture_bias,
    router_weight,
    expert_up,
    expert_down,
):
    local_rows = tokens.shape[0]
    width = tokens.shape[1]
    experts = router_weight.shape[1]
    owners = lax.axis_size("expert")
    per_owner = expert_up.shape[0]
    capacity = 2 * TOP * local_rows // experts
    images = local_rows // SEQ
    heads = width // HEAD_DIM
    scale = 1.0 / HEAD_DIM**0.5
    spread_rows = owners * capacity
    gain_one, bias_one, triple, merge_full, gain_two, bias_two, router = (
        lax.all_gather(attend_gain.astype(jnp.bfloat16), "fsdp", axis=0, tiled=True),
        lax.all_gather(attend_bias.astype(jnp.bfloat16), "fsdp", axis=0, tiled=True),
        lax.all_gather(triple_weight.astype(jnp.bfloat16), "fsdp", axis=0, tiled=True),
        lax.all_gather(merge_weight.astype(jnp.bfloat16), "fsdp", axis=0, tiled=True),
        lax.all_gather(mixture_gain.astype(jnp.bfloat16), "fsdp", axis=0, tiled=True),
        lax.all_gather(mixture_bias.astype(jnp.bfloat16), "fsdp", axis=0, tiled=True),
        lax.all_gather(router_weight.astype(jnp.bfloat16), "fsdp", axis=0, tiled=True),
    )
    up_full, down_full = (
        lax.all_gather(expert_up.astype(jnp.bfloat16), "fsdp", axis=1, tiled=True),
        lax.all_gather(expert_down.astype(jnp.bfloat16), "fsdp", axis=1, tiled=True),
    )
    inputs = tokens.astype(jnp.float32)
    normed_one, norm_back_one = jax.vjp(
        layer_norm, inputs, gain_one.astype(jnp.float32), bias_one.astype(jnp.float32)
    )
    normed_low = normed_one.astype(jnp.bfloat16)
    joined = jnp.dot(normed_low, triple, preferred_element_type=jnp.float32).astype(jnp.bfloat16)
    joined = joined.reshape(images, SEQ, 3, heads, HEAD_DIM)
    query_rows = joined[:, :, 0]
    key_rows = joined[:, :, 1]
    value_rows = joined[:, :, 2]
    scores = (
        jnp.einsum("bqhd,bkhd->bhqk", query_rows, key_rows, preferred_element_type=jnp.float32)
        * scale
    )
    top_score = jnp.max(scores, -1, keepdims=True)
    log_total = top_score + jnp.log(jnp.sum(jnp.exp(scores - top_score), -1, keepdims=True))
    weights_low = jnp.exp(scores - log_total).astype(jnp.bfloat16)
    mixed = jnp.einsum(
        "bhqk,bkhd->bqhd", weights_low, value_rows, preferred_element_type=jnp.float32
    )
    mixed = mixed.astype(jnp.bfloat16).reshape(local_rows, width)
    branch = jnp.dot(mixed, merge_full, preferred_element_type=jnp.float32)
    hidden_one = inputs + branch
    normed_two, norm_back_two = jax.vjp(
        layer_norm, hidden_one, gain_two.astype(jnp.float32), bias_two.astype(jnp.float32)
    )
    send_rows = normed_two.astype(jnp.bfloat16)
    logits = jnp.dot(send_rows, router, preferred_element_type=jnp.float32)
    probs = jax.nn.softmax(logits, -1)
    expert_ids = jnp.arange(experts, dtype=jnp.int32)
    picked = (routes[:, :, None] == expert_ids).astype(jnp.float32)
    gates = jnp.sum(picked * probs[:, None, :], 2)
    chosen = routes.reshape(-1)
    onehot = (chosen[:, None] == expert_ids).astype(jnp.int32)
    before = jnp.cumsum(onehot, 0) - onehot
    ranking = jnp.sum(before * onehot, 1)
    slots = chosen * capacity + ranking
    pair_ids = jnp.arange(chosen.shape[0], dtype=jnp.int32)
    filler = jnp.zeros((experts * capacity,), jnp.int32).at[slots].set(pair_ids + 1)
    token_source = jnp.where(filler > 0, (filler - 1) // TOP + 1, 0)
    padded = jnp.concatenate([jnp.zeros((1, width), jnp.bfloat16), send_rows], 0)
    outgoing = padded[token_source].reshape(owners, per_owner, capacity, width)
    arrived = lax.all_to_all(outgoing, "expert", split_axis=0, concat_axis=2, tiled=True).reshape(
        per_owner, spread_rows, width
    )
    hidden_list = []
    active_list = []
    result_list = []
    for member in range(per_owner):
        hidden_pre = jnp.dot(arrived[member], up_full[member], preferred_element_type=jnp.float32)
        activated = jax.nn.gelu(hidden_pre, approximate=False).astype(jnp.bfloat16)
        hidden_list.append(hidden_pre)
        active_list.append(activated)
        result_list.append(
            jnp.dot(activated, down_full[member], preferred_element_type=jnp.float32).astype(
                jnp.bfloat16
            )
        )
    expert_out = jnp.stack(result_list, 0).reshape(1, per_owner, spread_rows, width)
    returned = lax.all_to_all(expert_out, "expert", split_axis=2, concat_axis=0, tiled=True)
    pair_out = (
        returned.reshape(experts * capacity, width)[slots]
        .reshape(local_rows, TOP, width)
        .astype(jnp.float32)
    )
    mixture = jnp.sum(gates[:, :, None] * pair_out, 1)
    block_out = (hidden_one + mixture).astype(jnp.bfloat16)
    upstream = cotangent.astype(jnp.float32)
    gate_grad = jnp.sum(upstream[:, None, :] * pair_out, 2)
    pair_grad = (
        (gates[:, :, None] * upstream[:, None, :])
        .astype(jnp.bfloat16)
        .reshape(local_rows * TOP, width)
    )
    padded_grad = jnp.concatenate([jnp.zeros((1, width), jnp.bfloat16), pair_grad], 0)
    outgoing_grad = padded_grad[filler].reshape(owners, per_owner, capacity, width)
    arrived_grad = lax.all_to_all(
        outgoing_grad, "expert", split_axis=0, concat_axis=2, tiled=True
    ).reshape(per_owner, spread_rows, width)
    up_back, down_back = (
        lax.all_gather(expert_up.astype(jnp.bfloat16), "fsdp", axis=1, tiled=True),
        lax.all_gather(expert_down.astype(jnp.bfloat16), "fsdp", axis=1, tiled=True),
    )
    up_list = []
    down_list = []
    row_list = []
    for member in range(per_owner):
        act_grad = jnp.dot(
            arrived_grad[member], down_back[member].T, preferred_element_type=jnp.float32
        )
        down_list.append(
            jnp.dot(active_list[member].T, arrived_grad[member], preferred_element_type=jnp.float32)
        )
        gelu_back = jax.vjp(partial(jax.nn.gelu, approximate=False), hidden_list[member])[1]
        pre_grad = gelu_back(act_grad)[0].astype(jnp.bfloat16)
        up_list.append(jnp.dot(arrived[member].T, pre_grad, preferred_element_type=jnp.float32))
        row_list.append(
            jnp.dot(pre_grad, up_back[member].T, preferred_element_type=jnp.float32).astype(
                jnp.bfloat16
            )
        )
    row_grad = jnp.stack(row_list, 0).reshape(1, per_owner, spread_rows, width)
    back_rows = lax.all_to_all(row_grad, "expert", split_axis=2, concat_axis=0, tiled=True)
    send_grad = jnp.sum(
        back_rows.reshape(experts * capacity, width)[slots]
        .reshape(local_rows, TOP, width)
        .astype(jnp.float32),
        1,
    )
    up_total = jnp.stack(up_list, 0)
    down_total = jnp.stack(down_list, 0)
    expertup_grad, expertdown_grad = (
        lax.psum_scatter(
            up_total.astype(jnp.bfloat16), "fsdp", scatter_dimension=1, tiled=True
        ).astype(jnp.float32),
        lax.psum_scatter(
            down_total.astype(jnp.bfloat16), "fsdp", scatter_dimension=1, tiled=True
        ).astype(jnp.float32),
    )
    prob_grad = jnp.sum(picked * gate_grad[:, :, None], 1)
    logit_grad = (probs * (prob_grad - jnp.sum(probs * prob_grad, -1, keepdims=True))).astype(
        jnp.bfloat16
    )
    router_term = jnp.dot(send_rows.T, logit_grad, preferred_element_type=jnp.float32)
    normed_grad = send_grad + jnp.dot(logit_grad, router.T, preferred_element_type=jnp.float32)
    hidden_grad, gain_two_term, bias_two_term = norm_back_two(normed_grad)
    hidden_grad = hidden_grad + upstream
    branch_grad = hidden_grad.astype(jnp.bfloat16)
    merge_term = jnp.dot(mixed.T, branch_grad, preferred_element_type=jnp.float32)
    mixed_grad = jnp.dot(branch_grad, merge_full.T, preferred_element_type=jnp.float32).astype(
        jnp.bfloat16
    )
    mixed_grad = mixed_grad.reshape(images, SEQ, heads, HEAD_DIM)
    scores_again = (
        jnp.einsum("bqhd,bkhd->bhqk", query_rows, key_rows, preferred_element_type=jnp.float32)
        * scale
    )
    probs_again = jnp.exp(scores_again - log_total)
    weight_grad = jnp.einsum(
        "bqhd,bkhd->bhqk", mixed_grad, value_rows, preferred_element_type=jnp.float32
    )
    score_grad = (
        probs_again * (weight_grad - jnp.sum(probs_again * weight_grad, -1, keepdims=True))
    ).astype(jnp.bfloat16)
    query_grad = (
        jnp.einsum("bhqk,bkhd->bqhd", score_grad, key_rows, preferred_element_type=jnp.float32)
        * scale
    )
    key_grad = (
        jnp.einsum("bhqk,bqhd->bkhd", score_grad, query_rows, preferred_element_type=jnp.float32)
        * scale
    )
    value_grad = jnp.einsum(
        "bhqk,bqhd->bkhd",
        probs_again.astype(jnp.bfloat16),
        mixed_grad,
        preferred_element_type=jnp.float32,
    )
    joined_grad = (
        jnp.stack([query_grad, key_grad, value_grad], 2)
        .astype(jnp.bfloat16)
        .reshape(local_rows, 3 * width)
    )
    triple_term = jnp.dot(normed_low.T, joined_grad, preferred_element_type=jnp.float32)
    normed_one_grad = jnp.dot(joined_grad, triple.T, preferred_element_type=jnp.float32)
    input_grad, gain_one_term, bias_one_term = norm_back_one(normed_one_grad)
    tokens_grad = input_grad + hidden_grad
    shares = (
        lax.psum_scatter(
            gain_one_term.astype(jnp.bfloat16), "fsdp", scatter_dimension=0, tiled=True
        ).astype(jnp.float32),
        lax.psum_scatter(
            bias_one_term.astype(jnp.bfloat16), "fsdp", scatter_dimension=0, tiled=True
        ).astype(jnp.float32),
        lax.psum_scatter(
            triple_term.astype(jnp.bfloat16), "fsdp", scatter_dimension=0, tiled=True
        ).astype(jnp.float32),
        lax.psum_scatter(
            merge_term.astype(jnp.bfloat16), "fsdp", scatter_dimension=0, tiled=True
        ).astype(jnp.float32),
        lax.psum_scatter(
            gain_two_term.astype(jnp.bfloat16), "fsdp", scatter_dimension=0, tiled=True
        ).astype(jnp.float32),
        lax.psum_scatter(
            bias_two_term.astype(jnp.bfloat16), "fsdp", scatter_dimension=0, tiled=True
        ).astype(jnp.float32),
        lax.psum_scatter(
            router_term.astype(jnp.bfloat16), "fsdp", scatter_dimension=0, tiled=True
        ).astype(jnp.float32),
    )
    totals = (
        lax.psum(shares[0].astype(jnp.bfloat16), "expert").astype(jnp.float32),
        lax.psum(shares[1].astype(jnp.bfloat16), "expert").astype(jnp.float32),
        lax.psum(shares[2].astype(jnp.bfloat16), "expert").astype(jnp.float32),
        lax.psum(shares[3].astype(jnp.bfloat16), "expert").astype(jnp.float32),
        lax.psum(shares[4].astype(jnp.bfloat16), "expert").astype(jnp.float32),
        lax.psum(shares[5].astype(jnp.bfloat16), "expert").astype(jnp.float32),
        lax.psum(shares[6].astype(jnp.bfloat16), "expert").astype(jnp.float32),
    )
    return (
        block_out,
        tokens_grad,
        totals[0],
        totals[1],
        totals[2],
        totals[3],
        totals[4],
        totals[5],
        totals[6],
        expertup_grad,
        expertdown_grad,
    )


def solution(mesh):
    return jax.shard_map(
        local,
        mesh=mesh,
        in_specs=(
            P(("expert", "fsdp"), None),
            P(("expert", "fsdp"), None),
            P(("expert", "fsdp"), None),
            P("fsdp"),
            P("fsdp"),
            P("fsdp", None),
            P("fsdp", None),
            P("fsdp"),
            P("fsdp"),
            P("fsdp", None),
            P("expert", "fsdp", None),
            P("expert", "fsdp", None),
        ),
        out_specs=(
            P(("expert", "fsdp"), None),
            P(("expert", "fsdp"), None),
            P("fsdp"),
            P("fsdp"),
            P("fsdp", None),
            P("fsdp", None),
            P("fsdp"),
            P("fsdp"),
            P("fsdp", None),
            P("expert", "fsdp", None),
            P("expert", "fsdp", None),
        ),
        check_vma=False,
    )
```

profile of v0, /device:TPU:0, one launch (start us, length us, event | category | flops | bytes accessed | tf_op | source)
XLA Modules:
  0.0 934.5 jit_solution(5010760115874107428)
XLA Ops:
  15.2 15.2 %all-reduce.12 = (bf16[512]{0:T(512)(128)(2,1)S(1)}, bf16[512]{0:T(512)(128)(2,1)S(1)}, bf16[512]{0:T(512)(128)(2,1)S(1)}, bf16[512]{0:T(512)(128)(2,1)S(1)}) all-reduce(bf16[512]{0:T(512)(128)(2,1)S(1)} %dynamic-update-slice.1, bf16[512]{0:T(512)(128)(2,1)S(1)} %dynamic-update-slice, ...), channel_id=1, replica_groups=mesh['expert'=4,'fsdp'=8] {'fsdp'}, use_global_device_ids=true, to_apply=%add.4 | all-reduce | flops 2048 | bytes 8192
  30.5 8.1 all-gather
  44.7 3.6 mul.290
  48.4 5.4 mul.291
  53.9 8.8 scatter_custom_fusion
  62.7 10.8 %all_gather.32 = bf16[512,512]{1,0:T(8,128)(2,1)} all-gather(bf16[64,512]{1,0:T(8,128)(2,1)S(1)} %convert_element_type.210), channel_id=1, replica_groups=mesh['expert'=4,'fsdp'=8] {'fsdp'}, dimensions={0}, use_global_device_ids=true | all-gather | bytes 589824 | tf_op jit(solution)/shard_map/all_gather | solution.py:47
  74.3 3.0 convolution_convert_fusion
  77.3 4.9 reshape.293
  82.2 4.7 fusion.72
  89.1 3.2 copy.155
  108.7 10.3 %gather_fusion.2 = bf16[3152,512]{1,0:T(8,128)(2,1)} fusion(bf16[1577,512]{1,0:T(8,128)(2,1)S(1)} %concatenate.7, s32[4096]{0:T(1024)S(1)} %get-tuple-element.65), kind=kCustom, calls=%fused_computation.2 | custom fusion | bytes 6467904 | tf_op jit(solution)/shard_map/gather | solution.py:131
  118.9 2.7 reshape.216
  121.7 5.0 copy.127
  126.7 5.0 all-to-all-start.2
  132.7 10.2 %gather_fusion = bf16[3152,512]{1,0:T(8,128)(2,1)} fusion(bf16[789,512]{1,0:T(8,128)(2,1)S(1)} %concatenate.6, s32[4096]{0:T(1024)S(1)} %get-tuple-element.66), kind=kCustom, calls=%fused_computation | custom fusion | bytes 6467904 | tf_op jit(solution)/shard_map/gather | solution.py:97
  145.5 5.0 copy.122
  150.5 54.2 %all-to-all-done.2 = bf16[4,2,394,512]{3,1,2,0:T(2,128)(2,1)} async-done(((bf16[4,2,394,512]{3,1,2,0:T(2,128)(2,1)}), bf16[4,2,394,512]{3,1,2,0:T(2,128)(2,1)}, u32[]{:S(2)}, u32[]{:S(2)}) %all-to-all-start.2) | async-done | bytes 3227680 | tf_op jit(solution)/shard_map/all_to_all | solution.py:132
  204.7 3.7 all-to-all-start
  210.6 37.3 %slice_reduce_fusion.1 = (bf16[4,394,512]{2,1,0:T(8,128)(2,1)}, bf16[4,394,512]{2,1,0:T(8,128)(2,1)}) fusion(bf16[1,2,4,394,512]{4,1,3,2,0:T(2,128)(2,1)} %bitcast.21), kind=kLoop, calls=%fused_computation.51 | loop fusion | bytes 6455296 | tf_op jit(solution)/shard_map/slice | solution.py:144
  248.0 3.0 squeeze.50
  251.0 3.0 squeeze.51
  254.0 26.5 %all-to-all-done = bf16[4,2,394,512]{3,1,2,0:T(2,128)(2,1)S(1)} async-done(((bf16[4,2,394,512]{3,1,2,0:T(2,128)(2,1)}), bf16[4,2,394,512]{3,1,2,0:T(2,128)(2,1)S(1)}, u32[]{:S(2)}, u32[]{:S(2)}) %all-to-all-start) | async-done | bytes 3227680 | tf_op jit(solution)/shard_map/all_to_all | solution.py:98
  280.6 36.0 %slice_reduce_fusion.3 = (bf16[4,394,512]{2,1,0:T(8,128)(2,1)}, bf16[4,394,512]{2,1,0:T(8,128)(2,1)}) fusion(bf16[1,2,4,394,512]{4,1,3,2,0:T(2,128)(2,1)S(1)} %bitcast.150), kind=kLoop, calls=%fused_computation.53 | loop fusion | bytes 6455296 | tf_op jit(solution)/shard_map/slice | solution.py:105
  320.2 32.9 %multiply_convert_fusion = (bf16[1576,2048]{1,0:T(8,128)(2,1)}, f32[1576,2048]{1,0:T(8,128)}, f32[1576,2048]{1,0:T(8,128)}) fusion(bf16[1576,512]{1,0:T(8,128)(2,1)} %squeeze.47, bf16[2,512,2048]{2,1,0:T(8,128)(2,1)} %all-gather.7.cloned.1.call-done), kind=kOutput, calls=%fused_computation.11 | convolution fusion | flops 3514908672 | bytes 35987456 | tf_op jit(solution)/shard_map/dot_general | solution.py:105
  353.2 15.5 %add_convert_fusion = bf16[1576,2048]{1,0:T(8,128)(2,1)} fusion(f32[1576,2048]{1,0:T(8,128)} %get-tuple-element.44, f32[1576,2048]{1,0:T(8,128)} %get-tuple-element.57, bf16[1576,512]{1,0:T(8,128)(2,1)S(1)} %copy-done.26, bf16[2,2048,512]{2,1,0:T(8,128)(2,1)} %all-gather.9.cloned.1.call-done), kind=kOutput, calls=%fused_computation.9 | convolution fusion | flops 3350298624 | bytes 35987456 | tf_op jit(solution)/shard_map/dot_general | solution.py:143
  368.6 6.4 fusion.16
  375.1 32.5 %multiply_convert_fusion.1 = (bf16[1576,2048]{1,0:T(8,128)(2,1)}, f32[1576,2048]{1,0:T(8,128)}, f32[1576,2048]{1,0:T(8,128)}) fusion(bf16[1576,512]{1,0:T(8,128)(2,1)S(1)} %squeeze.44, bf16[2,512,2048]{2,1,0:T(8,128)(2,1)S(1)} %copy-done.62), kind=kOutput, calls=%fused_computation.24 | convolution fusion | flops 3514908672 | bytes 35987456 | tf_op jit(solution)/shard_map/dot_general | solution.py:105
  407.6 15.6 %add_convert_fusion.1 = bf16[1576,2048]{1,0:T(8,128)(2,1)} fusion(f32[1576,2048]{1,0:T(8,128)} %get-tuple-element.42, f32[1576,2048]{1,0:T(8,128)} %get-tuple-element.60, bf16[1576,512]{1,0:T(8,128)(2,1)S(1)} %copy-done.24, bf16[2,2048,512]{2,1,0:T(8,128)(2,1)} %all-gather.9.cloned.1.call-done), kind=kOutput, calls=%fused_computation.10 | convolution fusion | flops 3350298624 | bytes 35987456 | tf_op jit(solution)/shard_map/dot_general | solution.py:143
  423.2 6.4 fusion.15
  429.9 11.9 %copy.128 = bf16[1,2,1576,512]{3,1,0,2:T(2,128)(2,1)} copy(bf16[1,2,1576,512]{3,2,1,0:T(8,128)(2,1)S(1)} %maximum_bitcast_fusion.1) | data formatting | bytes 6455296 | tf_op jit(solution)/shard_map/reshape | solution.py:157
  441.8 3.9 all-to-all-start.3
  445.7 7.1 fusion.14
  452.8 6.4 fusion.13
  459.5 11.9 %copy.123 = bf16[1,2,1576,512]{3,1,0,2:T(2,128)(2,1)} copy(bf16[1,2,1576,512]{3,2,1,0:T(8,128)(2,1)S(1)} %maximum_bitcast_fusion) | data formatting | bytes 6455296 | tf_op jit(solution)/shard_map/reshape | solution.py:114
  471.4 46.3 %all-to-all-done.3 = bf16[1,2,1576,512]{3,1,0,2:T(2,128)(2,1)S(1)} async-done(((bf16[1,2,1576,512]{3,1,0,2:T(2,128)(2,1)}), bf16[1,2,1576,512]{3,1,0,2:T(2,128)(2,1)S(1)}, u32[]{:S(2)}, u32[]{:S(2)}) %all-to-all-start.3) | async-done | bytes 3227680 | tf_op jit(solution)/shard_map/all_to_all | solution.py:158
  517.7 4.7 all-to-all-start.1
  527.4 2.6 reshape.218
  530.0 64.4 %all-to-all-done.1 = bf16[1,2,1576,512]{3,1,0,2:T(2,128)(2,1)} async-done(((bf16[1,2,1576,512]{3,1,0,2:T(2,128)(2,1)}), bf16[1,2,1576,512]{3,1,0,2:T(2,128)(2,1)}, u32[]{:S(2)}, u32[]{:S(2)}) %all-to-all-start.1) | async-done | bytes 3227680 | tf_op jit(solution)/shard_map/all_to_all | solution.py:115
  598.8 3.6 reshape.215
  602.3 6.0 gather_fusion.3
  608.3 8.4 gather_fusion.1
  616.8 3.6 reshape.221
  620.5 9.9 %multiply_reduce_fusion.2 = (f32[788,2]{1,0:T(8,128)}, f32[788,512]{1,0:T(8,128)}) fusion(f32[788,2,512]{2,1,0:T(2,128)S(1)} %reshape.221, f32[788,512]{1,0:T(8,128)} %convert_element_type.227, f32[788,2]{1,0:T(8,128)} %copy.118), kind=kLoop, calls=%fused_computation.56 | loop fusion | flops 2822616 | bytes 6467904 | tf_op jit(solution)/shard_map/reduce_sum | solution.py:124
  631.7 5.4 reshape.222
  637.1 5.8 reduce_sum.242
  654.8 4.2 fusion.35
  659.1 7.3 multiply_reduce_fusion
  666.7 6.4 multiply_convert_fusion.2
  675.8 4.5 copy.138
  680.3 6.8 convert_element_type.239
  687.2 5.2 convolution_convert_fusion.5
  692.4 8.9 fusion.18
  701.3 8.2 fusion.17
  710.6 4.7 pad_maximum_fusion
  715.6 7.4 fusion.20
  723.0 7.5 fusion.19
  733.6 4.3 fusion.68
  740.1 12.1 %all-reduce.11 = (bf16[512]{0:T(512)(128)(2,1)S(1)}, bf16[512]{0:T(512)(128)(2,1)S(1)}, bf16[512]{0:T(512)(128)(2,1)S(1)}, bf16[512]{0:T(512)(128)(2,1)S(1)}) all-reduce(bf16[512]{0:T(512)(128)(2,1)S(1)} %get-tuple-element.19, bf16[512]{0:T(512)(128)(2,1)S(1)} %get-tuple-element.22, ...), channel_id=2, replica_groups=mesh['expert'=4,'fsdp'=8] {'fsdp'}, use_global_device_ids=true, to_apply=%region_24.25.clone | all-reduce | flops 2048 | bytes 8192
  752.5 3.2 add_add_fusion.2
  755.7 21.6 %reduce-scatter.16.cloned.1.call-done = bf16[64,8]{1,0:T(8,128)(2,1)} async-done(((bf16[512,8]{1,0:T(8,128)(2,1)}), bf16[64,8]{1,0:T(8,128)(2,1)}) %reduce-scatter.16.cloned.1.call-update) | async-done | bytes 1040
  778.1 11.7 %all-reduce.13 = (bf16[64]{0:T(256)(128)(2,1)S(1)}, bf16[64]{0:T(256)(128)(2,1)S(1)}, bf16[64]{0:T(256)(128)(2,1)S(1)}, bf16[64]{0:T(256)(128)(2,1)S(1)}, bf16[64,8]{0,1:T(8,128)(2,1)S(1)}) all-reduce(bf16[64]{0:T(256)(128)(2,1)S(1)} %dynamic-slice.5, ...), channel_id=1, replica_groups=mesh['expert'=4,'fsdp'=8] {'expert'}, use_global_device_ids=true, to_apply=%region_25.26 | all-reduce | flops 768 | bytes 3072 | tf_op jit(solution)/shard_map/psum | solution.py:247
  792.5 39.4 %reduce-scatter.12.cloned.1.call-done = bf16[2,64,2048]{2,1,0:T(8,128)(2,1)} async-done(((bf16[2,512,2048]{2,1,0:T(8,128)(2,1)}), bf16[2,64,2048]{2,1,0:T(8,128)(2,1)}) %reduce-scatter.12.cloned.1.call-update) | async-done | bytes 524304 | tf_op jit(solution)/shard_map/reduce_scatter | solution.py:168
  834.0 52.4 %reduce-scatter.14.cloned.1.call-done = bf16[2,256,512]{2,1,0:T(8,128)(2,1)} async-done(((bf16[2,2048,512]{2,1,0:T(8,128)(2,1)}), bf16[2,256,512]{2,1,0:T(8,128)(2,1)}) %reduce-scatter.14.cloned.1.call-update) | async-done | bytes 524304 | tf_op jit(solution)/shard_map/reduce_scatter | solution.py:171
  888.5 35.9 %all-reduce.17.cloned.1.call-done = (bf16[64,1536]{1,0:T(8,128)(2,1)}, bf16[64,512]{1,0:T(8,128)(2,1)}) async-done(((bf16[64,1536]{1,0:T(8,128)(2,1)}, bf16[64,512]{1,0:T(8,128)(2,1)}), (bf16[64,1536]{1,0:T(8,128)(2,1)}, bf16[64,512]{1,0:T(8,128)(2,1)})) %all-reduce.17.cloned.1.call-update) | async-done | bytes 262160 | tf_op jit(solution)/shard_map/psum | solution.py:249
  (265 shorter events, 85.2 us)
Async XLA Ops:
  7.2 67.1 %all-gather.5.cloned.1.call-start = ((), (), s32[]{:S(2)}) async-start(), calls=%async_computation.9 | async-start | bytes 1769472 | tf_op jit(solution)/shard_map/all_gather | solution.py:46
  30.4 43.9 %copy-start.60 = (f32[512]{0:T(512)}, f32[512]{0:T(512)S(1)}, u32[]{:S(2)}) copy-start(f32[512]{0:T(512)S(1)} %convert_element_type.203) | copy-start | bytes 6148
  30.4 43.9 %copy-start.58 = (f32[512]{0:T(512)}, f32[512]{0:T(512)S(1)}, u32[]{:S(2)}) copy-start(f32[512]{0:T(512)S(1)} %convert_element_type.201) | copy-start | bytes 6148
  30.4 72.3 %copy-start.54 = (f32[512]{0:T(512)}, f32[512]{0:T(512)S(1)}, u32[]{:S(2)}) copy-start(f32[512]{0:T(512)S(1)} %convert_element_type.212) | copy-start | bytes 6148
  38.6 65.2 %copy-start.40 = (bf16[512,8]{0,1:T(8,128)(2,1)}, bf16[512,8]{0,1:T(8,128)(2,1)S(1)}, u32[]{:S(2)}) copy-start(bf16[512,8]{0,1:T(8,128)(2,1)S(1)} %reshape.278) | copy-start | bytes 24580
  48.4 25.2 %copy-start.3 = (bf16[788,512]{1,0:T(8,128)(2,1)S(1)}, bf16[788,512]{1,0:T(8,128)(2,1)}, u32[]{:S(2)}) copy-start(bf16[788,512]{1,0:T(8,128)(2,1)} %param.12) | copy-start | bytes 2420740
  53.8 8.9 copy-start.56
  73.8 3.5 copy-start.46
  74.2 3.1 copy-start.48
  74.2 3.1 copy-start.52
  89.1 6.4 copy-start.11
  95.5 3.4 copy-start
  99.0 2.6 copy-start.22
  101.6 4.1 copy-start.34
  102.3 5.6 copy-start.8
  102.3 3.4 copy-start.36
  102.7 2.4 copy-start.50
  103.5 4.8 copy-start.42
  105.7 3.0 copy-start.44
  126.7 5.0 copy-start.29
  126.7 5.9 copy-start.6
  126.7 78.1 %all-to-all-start.2 = ((bf16[4,2,394,512]{3,1,2,0:T(2,128)(2,1)}), bf16[4,2,394,512]{3,1,2,0:T(2,128)(2,1)}, u32[]{:S(2)}, u32[]{:S(2)}) async-start(bf16[4,2,394,512]{3,1,2,0:T(2,128)(2,1)} %copy.127), calls=%async_computation.2 | async-start | bytes 6455296 | tf_op jit(solution)/shard_map/all_to_all | solution.py:132
  131.6 188.6 %all-gather.7.cloned.1.call-start = ((), (), s32[]{:S(2)}) async-start(), calls=%async_computation.10 | async-start | bytes 4718592 | tf_op jit(solution)/shard_map/all_gather | solution.py:53
  204.7 75.8 %all-to-all-start = ((bf16[4,2,394,512]{3,1,2,0:T(2,128)(2,1)}), bf16[4,2,394,512]{3,1,2,0:T(2,128)(2,1)S(1)}, u32[]{:S(2)}, u32[]{:S(2)}) async-start(bf16[4,2,394,512]{3,1,2,0:T(2,128)(2,1)} %copy.122), calls=%async_computation | async-start | bytes 6455296 | tf_op jit(solution)/shard_map/all_to_all | solution.py:98
  208.5 144.7 %all-gather.9.cloned.1.call-start = ((), (), s32[]{:S(2)}) async-start(), calls=%async_computation.11 | async-start | bytes 4718592 | tf_op jit(solution)/shard_map/all_gather | solution.py:54
  318.5 56.5 %copy-start.27 = (bf16[1576,512]{1,0:T(8,128)(2,1)}, bf16[1576,512]{1,0:T(8,128)(2,1)S(1)}, u32[]{:S(2)}) copy-start(bf16[1576,512]{1,0:T(8,128)(2,1)S(1)} %squeeze.44) | copy-start | bytes 4841476
  320.2 32.9 %copy-start.26 = (bf16[1576,512]{1,0:T(8,128)(2,1)S(1)}, bf16[1576,512]{1,0:T(8,128)(2,1)}, u32[]{:S(2)}) copy-start(bf16[1576,512]{1,0:T(8,128)(2,1)} %squeeze.51) | copy-start | bytes 4841476
  353.1 15.5 %copy-start.62 = (bf16[2,512,2048]{2,1,0:T(8,128)(2,1)S(1)}, bf16[2,512,2048]{2,1,0:T(8,128)(2,1)}, u32[]{:S(2)}) copy-start(bf16[2,512,2048]{2,1,0:T(8,128)(2,1)} %all-gather.7.cloned.1.call-done) | copy-start | bytes 12582916
  375.1 32.5 %copy-start.24 = (bf16[1576,512]{1,0:T(8,128)(2,1)S(1)}, bf16[1576,512]{1,0:T(8,128)(2,1)}, u32[]{:S(2)}) copy-start(bf16[1576,512]{1,0:T(8,128)(2,1)} %squeeze.50) | copy-start | bytes 4841476
  441.8 75.9 %all-to-all-start.3 = ((bf16[1,2,1576,512]{3,1,0,2:T(2,128)(2,1)}), bf16[1,2,1576,512]{3,1,0,2:T(2,128)(2,1)S(1)}, u32[]{:S(2)}, u32[]{:S(2)}) async-start(bf16[1,2,1576,512]{3,1,0,2:T(2,128)(2,1)} %copy.128), calls=%async_computation.3 | async-start | bytes 6455296 | tf_op jit(solution)/shard_map/all_to_all | solution.py:158
  445.7 7.2 copy-start.63
  471.4 53.5 %copy-start.57 = (s32[1576]{0:T(1024)S(1)}, s32[1576]{0:T(1024)}, u32[]{:S(2)}) copy-start(s32[1576]{0:T(1024)} %copy-done.56) | copy-start | bytes 18916
  517.7 76.7 %all-to-all-start.1 = ((bf16[1,2,1576,512]{3,1,0,2:T(2,128)(2,1)}), bf16[1,2,1576,512]{3,1,0,2:T(2,128)(2,1)}, u32[]{:S(2)}, u32[]{:S(2)}) async-start(bf16[1,2,1576,512]{3,1,0,2:T(2,128)(2,1)} %copy.123), calls=%async_computation.1 | async-start | bytes 6455296 | tf_op jit(solution)/shard_map/all_to_all | solution.py:115
  522.3 230.2 %reduce-scatter.10.cloned.1.call-start = ((), (), s32[]{:S(2)}) async-start(), calls=%async_computation.13 | async-start | bytes 589824 | tf_op jit(solution)/shard_map/reduce_scatter | solution.py:233
  620.4 11.1 %copy-start.35 = (s32[788,2]{0,1:T(2,128)S(1)}, s32[788,2]{0,1:T(2,128)}, u32[]{:S(2)}) copy-start(s32[788,2]{0,1:T(2,128)} %param.13) | copy-start | bytes 18916
  620.4 11.1 %copy-start.33 = (f32[788,8]{0,1:T(8,128)S(1)}, f32[788,8]{0,1:T(8,128)}, u32[]{:S(2)}) copy-start(f32[788,8]{0,1:T(8,128)} %copy-done.32) | copy-start | bytes 75652
  620.4 11.1 %copy-start.39 = (f32[788]{0:T(1024)S(1)}, f32[788]{0:T(1024)}, u32[]{:S(2)}) copy-start(f32[788]{0:T(1024)} %copy-done.38) | copy-start | bytes 9460
  620.5 11.1 %copy-start.45 = (f32[788]{0:T(1024)S(1)}, f32[788]{0:T(1024)}, u32[]{:S(2)}) copy-start(f32[788]{0:T(1024)} %copy-done.44) | copy-start | bytes 9460
  631.6 11.2 %copy-start.2 = (f32[788,512]{1,0:T(8,128)S(1)}, f32[788,512]{1,0:T(8,128)}, u32[]{:S(2)}) copy-start(f32[788,512]{1,0:T(8,128)} %copy-done.1) | copy-start | bytes 4841476
  631.7 11.2 %copy-start.37 = (f32[788]{0:T(1024)S(1)}, f32[788]{0:T(1024)}, u32[]{:S(2)}) copy-start(f32[788]{0:T(1024)} %copy-done.36) | copy-start | bytes 9460
  631.7 11.2 %copy-start.41 = (bf16[512,8]{0,1:T(8,128)(2,1)S(1)}, bf16[512,8]{0,1:T(8,128)(2,1)}, u32[]{:S(2)}) copy-start(bf16[512,8]{0,1:T(8,128)(2,1)} %copy-done.40) | copy-start | bytes 24580
  631.7 11.2 %copy-start.43 = (f32[788]{0:T(1024)S(1)}, f32[788]{0:T(1024)}, u32[]{:S(2)}) copy-start(f32[788]{0:T(1024)} %copy-done.42) | copy-start | bytes 9460
  631.7 11.2 %copy-start.55 = (f32[512]{0:T(512)S(1)}, f32[512]{0:T(512)}, u32[]{:S(2)}) copy-start(f32[512]{0:T(512)} %copy-done.54) | copy-start | bytes 6148
  637.1 6.8 copy-start.51
  643.9 3.2 copy-start.15
  643.9 3.2 copy-start.21
  644.4 4.3 copy-start.23
  648.7 6.1 copy-start.31
  654.8 4.3 copy-start.14
  666.5 86.0 %reduce-scatter.8.cloned.1.call-start = ((), (), s32[]{:S(2)}) async-start(), calls=%async_computation.12 | async-start | bytes 1769472 | tf_op jit(solution)/shard_map/reduce_scatter | solution.py:230
  666.7 6.4 copy-start.12
  680.3 6.8 copy-start.4
  680.3 6.8 copy-start.47
  680.3 6.8 copy-start.53
  680.3 6.8 copy-start.59
  680.3 6.8 copy-start.61
  692.4 85.0 %reduce-scatter.16.cloned.1.call-start = ((), (), s32[]{:S(2)}) async-start(), calls=%async_computation.16 | async-start | bytes 147456
  692.4 8.9 copy-start.28
  701.3 8.2 copy-start.7
  710.5 121.3 %reduce-scatter.12.cloned.1.call-start = ((), (), s32[]{:S(2)}) async-start(), calls=%async_computation.14 | async-start | bytes 4718592 | tf_op jit(solution)/shard_map/reduce_scatter | solution.py:168
  715.3 171.0 %reduce-scatter.14.cloned.1.call-start = ((), (), s32[]{:S(2)}) async-start(), calls=%async_computation.15 | async-start | bytes 4718592 | tf_op jit(solution)/shard_map/reduce_scatter | solution.py:171
  715.6 7.4 copy-start.25
  732.9 191.5 %all-reduce.17.cloned.1.call-start = ((), (), s32[]{:S(2)}) async-start(), calls=%async_computation.17 | async-start | bytes 524288 | tf_op jit(solution)/shard_map/psum | solution.py:249
  733.6 4.3 copy-start.49
  (13 other events, 15.9 us)
Sparse Core Ops, SparseCore 0:
  10.4 28.3 all-gather.4
  134.9 37.0 all-gather.6
  211.2 37.0 all-gather.8
  666.6 32.2 reduce-scatter.9
  702.0 38.3 reduce-scatter.7
  743.8 33.5 reduce-scatter.15
  780.7 51.1 reduce-scatter.11
  835.2 51.0 reduce-scatter.13
  888.7 35.6 all-reduce.16
where the time goes:
time: 945 us; the launch traced here: 935 us
  waiting for transfers between devices  341 us (36%)
  local copies, waits for them, and re-layouts  248 us (26%)
  matrix products  189 us (20%)
  other arithmetic  64 us (7%)
  blocking collectives  57.9 us (6%)
  starting transfers between devices  18 us (2%)
  between operations  16.7 us (2%)
    dot_general x2, matrix products, local(): jnp.dot(arrived[member], up_full[member], preferred_element_type=jnp.floa...  65.4 us
    all_to_all x1, waiting for transfers between devices, local(): lax.all_to_all(expert_out, 'expert', split_axis=2, concat_axis=0, tiled=T...  64.4 us
    all_to_all x1, waiting for transfers between devices, local(): lax.all_to_all(outgoing_grad, 'expert', split_axis=0, concat_axis=2, tile...  54.2 us
    reduce_scatter x1, waiting for transfers between devices, local(): lax.psum_scatter(down_total.astype(jnp.bfloat16), 'fsdp', scatter_dimensi...  52.4 us
    all_to_all x1, waiting for transfers between devices, local(): lax.all_to_all(row_grad, 'expert', split_axis=2, concat_axis=0, tiled=True)  46.3 us
    reduce_scatter x1, waiting for transfers between devices, local(): lax.psum_scatter(up_total.astype(jnp.bfloat16), 'fsdp', scatter_dimension...  39.4 us
    slice x1, local copies, waits for them, and re-layouts, local(): arrived_grad[member]  37.3 us
    slice x1, local copies, waits for them, and re-layouts, local(): arrived[member]  36 us
  transfers between devices with their start and end apart: 13, of which 8 were waited for; matrix products, arithmetic and copies ran while one was open for 30% of the time, Pallas kernels for 0%

commit v1 on v0

--- a/solution.py
+++ b/solution.py
@@ -8,6 +8,22 @@
 TOP = 2
 SEQ = 197
 EPSILON = 1e-06
+
+
+def exchange_in_pairs(x, axis, split, join):
+    ways, here = (lax.axis_size(axis), lax.axis_index(axis))
+    width = x.shape[split] // ways
+    shape = list(x.shape)
+    shape[split] = width
+    height = shape[join]
+    shape[join] = height * ways
+    full = jnp.zeros(shape, x.dtype)
+    for mask in range(ways):
+        part = lax.dynamic_slice_in_dim(x, (here ^ mask) * width, width, axis=split)
+        if mask:
+            part = lax.ppermute(part, axis, [(d, d ^ mask) for d in range(ways)])
+        full = lax.dynamic_update_slice_in_dim(full, part, (here ^ mask) * height, axis=join)
+    return full
 
 
 def layer_norm(values, gain, bias):
@@ -112,7 +128,7 @@
             )
         )
     expert_out = jnp.stack(result_list, 0).reshape(1, per_owner, spread_rows, width)
-    returned = lax.all_to_all(expert_out, "expert", split_axis=2, concat_axis=0, tiled=True)
+    returned = exchange_in_pairs(expert_out, "expert", 2, 0)
     pair_out = (
         returned.reshape(experts * capacity, width)[slots]
         .reshape(local_rows, TOP, width)

time: 945 us -> 908 us (0.961)
  waiting for transfers between devices: 341 us -> 301 us
  blocking collectives: 57.9 us -> 69.4 us
    ppermute x0 -> x3, waiting for transfers between devices: none -> 95 us  [exchange_in_pairs(): part = lax.ppermute(part, axis, [(d, d ^ mask) for d in range(ways)])]
    all_to_all x1 -> x0, waiting for transfers between devices: 64.4 us -> none  [local(): lax.all_to_all(expert_out, 'expert', split_axis=2, concat_axis=0, tiled=T...]
    all_to_all x1, waiting for transfers between devices: 46.3 us -> 0.01 us  [local(): lax.all_to_all(row_grad, 'expert', split_axis=2, concat_axis=0, tiled=True)]
    unnamed x10, waiting for transfers between devices: 21.8 us -> 0.17 us
    reshape x1 -> x0, local copies, waits for them, and re-layouts: 11.9 us -> none  [local(): jnp.stack(result_list, 0).reshape(1, per_owner, spread_rows, width)]
    psum x1, blocking collectives: 11.7 us -> 22.9 us  [local(): lax.psum(shares[0].astype(jnp.bfloat16), 'expert').astype(jnp.float32)]
    unnamed x149 -> x179, local copies, waits for them, and re-layouts: 19.6 us -> 21.5 us
  transfers between devices with their start and end apart: 13 -> 15, of which waited for: 8 -> 7; matrix products, arithmetic and copies ran while one was open for 30% -> 38% of each run, Pallas kernels for 0% -> 0%
where the time goes in v1:
time: 908 us; the launch traced here: 897 us
  waiting for transfers between devices  301 us (33%)
  local copies, waits for them, and re-layouts  242 us (27%)
  matrix products  188 us (21%)
  blocking collectives  69.4 us (8%)
  other arithmetic  61.6 us (7%)
  starting transfers between devices  18.5 us (2%)
  between operations  16.8 us (2%)
    ppermute x3, waiting for transfers between devices, exchange_in_pairs(): part = lax.ppermute(part, axis, [(d, d ^ mask) for d in range(ways)])  95 us
    dot_general x2, matrix products, local(): jnp.dot(arrived[member], up_full[member], preferred_element_type=jnp.floa...  65.4 us
    all_to_all x1, waiting for transfers between devices, local(): lax.all_to_all(outgoing_grad, 'expert', split_axis=0, concat_axis=2, tile...  54.2 us
    reduce_scatter x1, waiting for transfers between devices, local(): lax.psum_scatter(down_total.astype(jnp.bfloat16), 'fsdp', scatter_dimensi...  52.4 us
    slice x1, local copies, waits for them, and re-layouts, local(): arrived_grad[member]  37.4 us
    reduce_scatter x1, waiting for transfers between devices, local(): lax.psum_scatter(up_total.astype(jnp.bfloat16), 'fsdp', scatter_dimension...  36.9 us
    psum x1, waiting for transfers between devices, local(): lax.psum(shares[2].astype(jnp.bfloat16), 'expert').astype(jnp.float32)  35.9 us
    slice x1, local copies, waits for them, and re-layouts, local(): arrived[member]  35.9 us
  transfers between devices with their start and end apart: 15, of which 7 were waited for; matrix products, arithmetic and copies ran while one was open for 38% of the time, Pallas kernels for 0%

profile of v1, /device:TPU:0, one launch (start us, length us, event | category | flops | bytes accessed | tf_op | source)
XLA Modules:
  0.0 897.4 jit_solution(3017280288860091068)
XLA Ops:
  15.2 15.3 %all-reduce.12 = (bf16[512]{0:T(512)(128)(2,1)S(1)}, bf16[512]{0:T(512)(128)(2,1)S(1)}, bf16[512]{0:T(512)(128)(2,1)S(1)}, bf16[512]{0:T(512)(128)(2,1)S(1)}) all-reduce(bf16[512]{0:T(512)(128)(2,1)S(1)} %dynamic-update-slice.1, bf16[512]{0:T(512)(128)(2,1)S(1)} %dynamic-update-slice, ...), channel_id=1, replica_groups=mesh['expert'=4,'fsdp'=8] {'fsdp'}, use_global_device_ids=true, to_apply=%add.4 | all-reduce | flops 2048 | bytes 8192
  30.5 8.1 all-gather
  44.8 2.5 mul.306
  47.3 5.4 mul.307
  52.8 8.8 scatter_custom_fusion
  61.7 10.8 %all_gather.32 = bf16[512,512]{1,0:T(8,128)(2,1)} all-gather(bf16[64,512]{1,0:T(8,128)(2,1)S(1)} %convert_element_type.210), channel_id=1, replica_groups=mesh['expert'=4,'fsdp'=8] {'fsdp'}, dimensions={0}, use_global_device_ids=true | all-gather | bytes 589824 | tf_op jit(solution)/shard_map/all_gather | solution.py:63
  73.3 3.0 convolution_convert_fusion
  76.3 4.9 reshape.293
  81.2 4.7 fusion.81
  88.1 3.2 copy.188
  108.3 10.3 %gather_fusion.2 = bf16[3152,512]{1,0:T(8,128)(2,1)} fusion(bf16[1577,512]{1,0:T(8,128)(2,1)S(1)} %concatenate.7, s32[4096]{0:T(1024)S(1)} %get-tuple-element.68), kind=kCustom, calls=%fused_computation.2 | custom fusion | bytes 6467904 | tf_op jit(solution)/shard_map/gather | solution.py:147
  118.6 2.6 reshape.216
  121.2 5.0 copy.161
  126.2 5.0 all-to-all-start.1
  132.2 10.2 %gather_fusion = bf16[3152,512]{1,0:T(8,128)(2,1)} fusion(bf16[789,512]{1,0:T(8,128)(2,1)S(1)} %concatenate.6, s32[4096]{0:T(1024)S(1)} %get-tuple-element.69), kind=kCustom, calls=%fused_computation | custom fusion | bytes 6467904 | tf_op jit(solution)/shard_map/gather | solution.py:113
  142.5 2.5 reshape.214
  145.0 5.0 copy.153
  150.0 54.2 %all-to-all-done.1 = bf16[4,2,394,512]{3,1,2,0:T(2,128)(2,1)} async-done(((bf16[4,2,394,512]{3,1,2,0:T(2,128)(2,1)}), bf16[4,2,394,512]{3,1,2,0:T(2,128)(2,1)}, u32[]{:S(2)}, u32[]{:S(2)}) %all-to-all-start.1) | async-done | bytes 3227680 | tf_op jit(solution)/shard_map/all_to_all | solution.py:148
  204.2 3.7 all-to-all-start
  210.1 37.4 %slice_reduce_fusion.1 = (bf16[4,394,512]{2,1,0:T(8,128)(2,1)}, bf16[4,394,512]{2,1,0:T(8,128)(2,1)}) fusion(bf16[1,2,4,394,512]{4,1,3,2,0:T(2,128)(2,1)} %bitcast.22), kind=kLoop, calls=%fused_computation.58 | loop fusion | bytes 6455296 | tf_op jit(solution)/shard_map/slice | solution.py:160
  247.6 3.0 squeeze.50
  250.6 3.1 squeeze.51
  253.7 26.4 %all-to-all-done = bf16[4,2,394,512]{3,1,2,0:T(2,128)(2,1)S(1)} async-done(((bf16[4,2,394,512]{3,1,2,0:T(2,128)(2,1)}), bf16[4,2,394,512]{3,1,2,0:T(2,128)(2,1)S(1)}, u32[]{:S(2)}, u32[]{:S(2)}) %all-to-all-start) | async-done | bytes 3227680 | tf_op jit(solution)/shard_map/all_to_all | solution.py:114
  280.0 35.9 %slice_reduce_fusion.2 = (bf16[4,394,512]{2,1,0:T(8,128)(2,1)}, bf16[4,394,512]{2,1,0:T(8,128)(2,1)}) fusion(bf16[1,2,4,394,512]{4,1,3,2,0:T(2,128)(2,1)S(1)} %bitcast.154), kind=kLoop, calls=%fused_computation.59 | loop fusion | bytes 6455296 | tf_op jit(solution)/shard_map/slice | solution.py:121
  319.7 32.9 %multiply_convert_fusion.1 = (bf16[1576,2048]{1,0:T(8,128)(2,1)}, f32[1576,2048]{1,0:T(8,128)}, f32[1576,2048]{1,0:T(8,128)}) fusion(bf16[1576,512]{1,0:T(8,128)(2,1)} %squeeze.44, bf16[2,512,2048]{2,1,0:T(8,128)(2,1)} %all-gather.7.cloned.1.call-done), kind=kOutput, calls=%fused_computation.24 | convolution fusion | flops 3514908672 | bytes 35987456 | tf_op jit(solution)/shard_map/dot_general | solution.py:121
  352.6 15.5 %add_convert_fusion.1 = bf16[1576,2048]{1,0:T(8,128)(2,1)} fusion(f32[1576,2048]{1,0:T(8,128)} %get-tuple-element.44, f32[1576,2048]{1,0:T(8,128)} %get-tuple-element.63, bf16[1576,512]{1,0:T(8,128)(2,1)S(1)} %copy-done.35, bf16[2,2048,512]{2,1,0:T(8,128)(2,1)} %all-gather.9.cloned.1.call-done), kind=kOutput, calls=%fused_computation.10 | convolution fusion | flops 3350298624 | bytes 35987456 | tf_op jit(solution)/shard_map/dot_general | solution.py:159
  368.0 6.4 fusion.15
  374.5 32.5 %multiply_convert_fusion = (bf16[1576,2048]{1,0:T(8,128)(2,1)}, f32[1576,2048]{1,0:T(8,128)}, f32[1576,2048]{1,0:T(8,128)}) fusion(bf16[1576,512]{1,0:T(8,128)(2,1)S(1)} %squeeze.47, bf16[2,512,2048]{2,1,0:T(8,128)(2,1)S(1)} %copy-done.74), kind=kOutput, calls=%fused_computation.11 | convolution fusion | flops 3514908672 | bytes 35987456 | tf_op jit(solution)/shard_map/dot_general | solution.py:121
  407.0 15.1 %add_convert_fusion = bf16[1576,2048]{1,0:T(8,128)(2,1)} fusion(f32[1576,2048]{1,0:T(8,128)} %get-tuple-element.42, f32[1576,2048]{1,0:T(8,128)} %get-tuple-element.60, bf16[1576,512]{1,0:T(8,128)(2,1)S(1)} %copy-done.37, bf16[2,2048,512]{2,1,0:T(8,128)(2,1)} %all-gather.9.cloned.1.call-done), kind=kOutput, calls=%fused_computation.9 | convolution fusion | flops 3350298624 | bytes 35987456 | tf_op jit(solution)/shard_map/dot_general | solution.py:159
  422.1 6.4 fusion.16
  428.9 11.9 %copy.162 = bf16[1,2,1576,512]{3,1,0,2:T(2,128)(2,1)} copy(bf16[1,2,1576,512]{3,2,1,0:T(8,128)(2,1)S(1)} %maximum_bitcast_fusion) | data formatting | bytes 6455296 | tf_op jit(solution)/shard_map/reshape | solution.py:173
  440.7 4.7 all-to-all-start.2
  445.9 7.1 fusion.13
  453.0 6.4 fusion.14
  465.3 2.4 collective-permute-start.1
  473.2 42.8 %collective-permute-done = bf16[1,2,394,512]{3,1,2,0:T(2,128)(2,1)} collective-permute-done((bf16[1,2,394,512]{3,1,2,0:T(2,128)(2,1)}, bf16[1,2,394,512]{3,1,2,0:T(2,128)(2,1)}, u32[]{:S(2)}, u32[]{:S(2)}) %collective-permute-start) | collective-permute-done | bytes 806944 | tf_op jit(solution)/shard_map/ppermute | solution.py:24
  518.1 52.2 %collective-permute-done.1 = bf16[1,2,394,512]{3,1,2,0:T(2,128)(2,1)} collective-permute-done((bf16[1,2,394,512]{3,1,2,0:T(2,128)(2,1)}, bf16[1,2,394,512]{3,1,2,0:T(2,128)(2,1)}, u32[]{:S(2)}, u32[]{:S(2)}) %collective-permute-start.1) | collective-permute-done | bytes 806944 | tf_op jit(solution)/shard_map/ppermute | solution.py:24
  574.6 2.5 reshape.215
  577.1 6.0 gather_fusion.1
  583.1 5.1 reshape.221
  588.2 11.3 %multiply_reduce_fusion.2 = (f32[788,2]{1,0:T(8,128)S(1)}, f32[788,512]{1,0:T(8,128)}) fusion(f32[788,2,512]{2,1,0:T(2,128)} %reshape.221, f32[788,512]{1,0:T(8,128)S(1)} %copy-done.24, f32[788,2]{1,0:T(8,128)S(1)} %copy-done.32), kind=kLoop, calls=%fused_computation.62 | loop fusion | flops 2822616 | bytes 6467904 | tf_op jit(solution)/shard_map/reduce_sum | solution.py:140
  601.0 2.5 copy.197
  605.4 2.6 reshape.218
  607.9 6.0 gather_fusion.3
  614.0 4.9 reshape.222
  618.9 5.9 reduce_sum.242
  631.9 5.3 fusion.35
  637.2 7.5 multiply_reduce_fusion
  644.6 4.6 multiply_convert_fusion.2
  656.1 4.5 copy.172
  660.6 7.2 convert_element_type.239
  667.8 5.2 convolution_convert_fusion.5
  673.1 7.6 fusion.17
  680.7 7.2 fusion.18
  691.6 7.8 fusion.19
  699.4 7.5 fusion.20
  706.9 2.3 pad_maximum_fusion.1
  710.9 3.9 fusion.77
  716.8 12.3 %all-reduce.11 = (bf16[512]{0:T(512)(128)(2,1)S(1)}, bf16[512]{0:T(512)(128)(2,1)S(1)}, bf16[512]{0:T(512)(128)(2,1)S(1)}, bf16[512]{0:T(512)(128)(2,1)S(1)}) all-reduce(bf16[512]{0:T(512)(128)(2,1)S(1)} %get-tuple-element.19, bf16[512]{0:T(512)(128)(2,1)S(1)} %get-tuple-element.22, ...), channel_id=2, replica_groups=mesh['expert'=4,'fsdp'=8] {'fsdp'}, use_global_device_ids=true, to_apply=%region_24.25.clone | all-reduce | flops 2048 | bytes 8192
  729.4 22.9 %all-reduce.13 = (bf16[64]{0:T(256)(128)(2,1)S(1)}, bf16[64]{0:T(256)(128)(2,1)S(1)}, bf16[64]{0:T(256)(128)(2,1)S(1)}, bf16[64]{0:T(256)(128)(2,1)S(1)}, bf16[64,8]{0,1:T(8,128)(2,1)S(1)}) all-reduce(bf16[64]{0:T(256)(128)(2,1)S(1)} %dynamic-slice.21, ...), channel_id=1, replica_groups=mesh['expert'=4,'fsdp'=8] {'expert'}, use_global_device_ids=true, to_apply=%region_25.26 | all-reduce | flops 768 | bytes 3072 | tf_op jit(solution)/shard_map/psum | solution.py:263
  755.0 3.0 add_add_fusion.2
  758.1 36.9 %reduce-scatter.12.cloned.1.call-done = bf16[2,64,2048]{2,1,0:T(8,128)(2,1)} async-done(((bf16[2,512,2048]{2,1,0:T(8,128)(2,1)}), bf16[2,64,2048]{2,1,0:T(8,128)(2,1)}) %reduce-scatter.12.cloned.1.call-update) | async-done | bytes 524304 | tf_op jit(solution)/shard_map/reduce_scatter | solution.py:184
  797.1 52.4 %reduce-scatter.14.cloned.1.call-done = bf16[2,256,512]{2,1,0:T(8,128)(2,1)} async-done(((bf16[2,2048,512]{2,1,0:T(8,128)(2,1)}), bf16[2,256,512]{2,1,0:T(8,128)(2,1)}) %reduce-scatter.14.cloned.1.call-update) | async-done | bytes 524304 | tf_op jit(solution)/shard_map/reduce_scatter | solution.py:187
  851.6 35.9 %all-reduce.17.cloned.1.call-done = (bf16[64,1536]{1,0:T(8,128)(2,1)}, bf16[64,512]{1,0:T(8,128)(2,1)}) async-done(((bf16[64,1536]{1,0:T(8,128)(2,1)}, bf16[64,512]{1,0:T(8,128)(2,1)}), (bf16[64,1536]{1,0:T(8,128)(2,1)}, bf16[64,512]{1,0:T(8,128)(2,1)})) %all-reduce.17.cloned.1.call-update) | async-done | bytes 262160 | tf_op jit(solution)/shard_map/psum | solution.py:265
  (305 shorter events, 92.9 us)
Async XLA Ops:
  7.2 37.6 %copy-start.14 = (bf16[788,512]{1,0:T(8,128)(2,1)S(1)}, bf16[788,512]{1,0:T(8,128)(2,1)}, u32[]{:S(2)}) copy-start(bf16[788,512]{1,0:T(8,128)(2,1)} %param.14) | copy-start | bytes 2420740
  7.2 66.1 %all-gather.5.cloned.1.call-start = ((), (), s32[]{:S(2)}) async-start(), calls=%async_computation.8 | async-start | bytes 1769472 | tf_op jit(solution)/shard_map/all_gather | solution.py:62
  30.5 42.8 %copy-start.72 = (f32[512]{0:T(512)}, f32[512]{0:T(512)S(1)}, u32[]{:S(2)}) copy-start(f32[512]{0:T(512)S(1)} %convert_element_type.203) | copy-start | bytes 6148
  30.5 42.8 %copy-start.70 = (f32[512]{0:T(512)}, f32[512]{0:T(512)S(1)}, u32[]{:S(2)}) copy-start(f32[512]{0:T(512)S(1)} %convert_element_type.201) | copy-start | bytes 6148
  30.5 71.9 %copy-start.66 = (f32[512]{0:T(512)}, f32[512]{0:T(512)S(1)}, u32[]{:S(2)}) copy-start(f32[512]{0:T(512)S(1)} %convert_element_type.212) | copy-start | bytes 6148
  38.7 64.8 %copy-start.52 = (bf16[512,8]{0,1:T(8,128)(2,1)}, bf16[512,8]{0,1:T(8,128)(2,1)S(1)}, u32[]{:S(2)}) copy-start(bf16[512,8]{0,1:T(8,128)(2,1)S(1)} %reshape.278) | copy-start | bytes 24580
  47.3 25.2 %copy-start.3 = (bf16[788,512]{1,0:T(8,128)(2,1)S(1)}, bf16[788,512]{1,0:T(8,128)(2,1)}, u32[]{:S(2)}) copy-start(bf16[788,512]{1,0:T(8,128)(2,1)} %param.12) | copy-start | bytes 2420740
  52.8 8.9 copy-start.68
  72.7 3.5 copy-start.58
  73.2 3.1 copy-start.60
  88.1 6.4 copy-start.10
  102.0 3.4 copy-start.46
  102.0 5.6 copy-start.8
  102.0 3.3 copy-start.48
  103.2 4.7 copy-start.54
  126.2 5.0 copy-start.41
  126.2 5.9 copy-start.6
  126.2 78.1 %all-to-all-start.1 = ((bf16[4,2,394,512]{3,1,2,0:T(2,128)(2,1)}), bf16[4,2,394,512]{3,1,2,0:T(2,128)(2,1)}, u32[]{:S(2)}, u32[]{:S(2)}) async-start(bf16[4,2,394,512]{3,1,2,0:T(2,128)(2,1)} %copy.161), calls=%async_computation.1 | async-start | bytes 6455296 | tf_op jit(solution)/shard_map/all_to_all | solution.py:148
  131.2 188.5 %all-gather.7.cloned.1.call-start = ((), (), s32[]{:S(2)}) async-start(), calls=%async_computation.9 | async-start | bytes 4718592 | tf_op jit(solution)/shard_map/all_gather | solution.py:69
  204.2 75.8 %all-to-all-start = ((bf16[4,2,394,512]{3,1,2,0:T(2,128)(2,1)}), bf16[4,2,394,512]{3,1,2,0:T(2,128)(2,1)S(1)}, u32[]{:S(2)}, u32[]{:S(2)}) async-start(bf16[4,2,394,512]{3,1,2,0:T(2,128)(2,1)} %copy.153), calls=%async_computation | async-start | bytes 6455296 | tf_op jit(solution)/shard_map/all_to_all | solution.py:114
  208.0 144.6 %all-gather.9.cloned.1.call-start = ((), (), s32[]{:S(2)}) async-start(), calls=%async_computation.10 | async-start | bytes 4718592 | tf_op jit(solution)/shard_map/all_gather | solution.py:70
  317.9 56.5 %copy-start.39 = (bf16[1576,512]{1,0:T(8,128)(2,1)}, bf16[1576,512]{1,0:T(8,128)(2,1)S(1)}, u32[]{:S(2)}) copy-start(bf16[1576,512]{1,0:T(8,128)(2,1)S(1)} %squeeze.47) | copy-start | bytes 4841476
  319.7 32.9 %copy-start.35 = (bf16[1576,512]{1,0:T(8,128)(2,1)S(1)}, bf16[1576,512]{1,0:T(8,128)(2,1)}, u32[]{:S(2)}) copy-start(bf16[1576,512]{1,0:T(8,128)(2,1)} %squeeze.50) | copy-start | bytes 4841476
  352.6 15.5 %copy-start.74 = (bf16[2,512,2048]{2,1,0:T(8,128)(2,1)S(1)}, bf16[2,512,2048]{2,1,0:T(8,128)(2,1)}, u32[]{:S(2)}) copy-start(bf16[2,512,2048]{2,1,0:T(8,128)(2,1)} %all-gather.7.cloned.1.call-done) | copy-start | bytes 12582916
  374.5 32.5 %copy-start.37 = (bf16[1576,512]{1,0:T(8,128)(2,1)S(1)}, bf16[1576,512]{1,0:T(8,128)(2,1)}, u32[]{:S(2)}) copy-start(bf16[1576,512]{1,0:T(8,128)(2,1)} %squeeze.51) | copy-start | bytes 4841476
  440.7 160.2 %all-to-all-start.2 = ((bf16[1,2,1576,512]{3,1,0,2:T(2,128)(2,1)}), bf16[1,2,1576,512]{3,1,0,2:T(2,128)(2,1)}, u32[]{:S(2)}, u32[]{:S(2)}) async-start(bf16[1,2,1576,512]{3,1,0,2:T(2,128)(2,1)} %copy.162), calls=%async_computation.2 | async-start | bytes 6455296 | tf_op jit(solution)/shard_map/all_to_all | solution.py:174
  445.4 264.7 %reduce-scatter.16.cloned.1.call-start = ((), (), s32[]{:S(2)}) async-start(), calls=%async_computation.15 | async-start | bytes 147456
  445.9 7.2 copy-start.75
  460.0 8.7 copy-start.15
  460.0 10.1 %copy-start.69 = (s32[1576]{0:T(1024)S(1)}, s32[1576]{0:T(1024)}, u32[]{:S(2)}) copy-start(s32[1576]{0:T(1024)} %copy-done.68) | copy-start | bytes 18916
  461.7 54.3 %collective-permute-start = (bf16[1,2,394,512]{3,1,2,0:T(2,128)(2,1)}, bf16[1,2,394,512]{3,1,2,0:T(2,128)(2,1)}, u32[]{:S(2)}, u32[]{:S(2)}) collective-permute-start(bf16[1,2,394,512]{3,1,2,0:T(2,128)(2,1)} %copy.154), channel_id=1, source_target_pairs={{0,8},{8,0},{16,24},{24,16},{1,9},{9,1},{17,25},{25,17},{2,10},{10... | collective-permute-start | bytes 2420744 | tf_op jit(solution)/shard_map/ppermute | solution.py:24
  465.3 105.0 %collective-permute-start.1 = (bf16[1,2,394,512]{3,1,2,0:T(2,128)(2,1)}, bf16[1,2,394,512]{3,1,2,0:T(2,128)(2,1)}, u32[]{:S(2)}, u32[]{:S(2)}) collective-permute-start(bf16[1,2,394,512]{3,1,2,0:T(2,128)(2,1)} %copy.156), channel_id=1, source_target_pairs={{0,16},{8,24},{16,0},{24,8},{1,17},{9,25},{17,1},{25,9},{2,18},{10... | collective-permute-start | bytes 2420744 | tf_op jit(solution)/shard_map/ppermute | solution.py:24
  468.6 103.9 %collective-permute-start.2 = (bf16[1,2,394,512]{3,1,2,0:T(2,128)(2,1)S(1)}, bf16[1,2,394,512]{3,1,2,0:T(2,128)(2,1)}, u32[]{:S(2)}, u32[]{:S(2)}) collective-permute-start(bf16[1,2,394,512]{3,1,2,0:T(2,128)(2,1)S(1)} %copy.158), channel_id=1, source_target_pairs={{0,24},{8,16},{16,8},{24,0},{1,25},{9,17},{17,9},{25,1},{2,26},{10... | collective-permute-start | bytes 2420744 | tf_op jit(solution)/shard_map/ppermute | solution.py:24
  583.1 5.1 copy-start.24
  583.1 5.1 copy-start.32
  588.2 11.6 %copy-start.47 = (s32[788,2]{0,1:T(2,128)S(1)}, s32[788,2]{0,1:T(2,128)}, u32[]{:S(2)}) copy-start(s32[788,2]{0,1:T(2,128)} %param.13) | copy-start | bytes 18916
  588.2 11.6 %copy-start.45 = (f32[788,8]{0,1:T(8,128)S(1)}, f32[788,8]{0,1:T(8,128)}, u32[]{:S(2)}) copy-start(f32[788,8]{0,1:T(8,128)} %copy-done.44) | copy-start | bytes 75652
  588.2 11.6 %copy-start.51 = (f32[788]{0:T(1024)S(1)}, f32[788]{0:T(1024)}, u32[]{:S(2)}) copy-start(f32[788]{0:T(1024)} %copy-done.50) | copy-start | bytes 9460
  588.2 11.6 %copy-start.57 = (f32[788]{0:T(1024)S(1)}, f32[788]{0:T(1024)}, u32[]{:S(2)}) copy-start(f32[788]{0:T(1024)} %copy-done.56) | copy-start | bytes 9460
  588.2 11.6 %copy-start.7 = (bf16[788,512]{1,0:T(8,128)(2,1)S(1)}, bf16[788,512]{1,0:T(8,128)(2,1)}, u32[]{:S(2)}) copy-start(bf16[788,512]{1,0:T(8,128)(2,1)} %copy-done.5) | copy-start | bytes 2420740
  600.9 154.1 %reduce-scatter.10.cloned.1.call-start = ((), (), s32[]{:S(2)}) async-start(), calls=%async_computation.12 | async-start | bytes 589824 | tf_op jit(solution)/shard_map/reduce_scatter | solution.py:249
  618.9 5.9 copy-start.2
  618.9 5.9 copy-start.49
  618.9 5.9 copy-start.53
  618.9 5.9 copy-start.55
  618.9 5.9 copy-start.67
  631.9 5.3 copy-start.13
  631.9 12.8 %slice-start = ((s8[6553600]{0:T(1024)(128)(4,1)}), s8[4194304]{0:T(1024)(128)(4,1)S(1)}, s32[]{:S(2)}) async-start(s8[6553600]{0:T(1024)(128)(4,1)} %bitcast.152), calls=%async_computation.17 | async-start | bytes 8388608
  637.2 7.5 slice-start.1
  644.6 4.6 copy-start.11
  653.1 101.9 %reduce-scatter.8.cloned.1.call-start = ((), (), s32[]{:S(2)}) async-start(), calls=%async_computation.11 | async-start | bytes 1769472 | tf_op jit(solution)/shard_map/reduce_scatter | solution.py:246
  660.5 7.2 copy-start.4
  660.6 7.2 copy-start.59
  660.6 7.2 copy-start.65
  660.6 7.2 copy-start.71
  660.6 7.2 copy-start.73
  673.0 7.7 copy-start.40
  673.0 121.9 %reduce-scatter.12.cloned.1.call-start = ((), (), s32[]{:S(2)}) async-start(), calls=%async_computation.13 | async-start | bytes 4718592 | tf_op jit(solution)/shard_map/reduce_scatter | solution.py:184
  690.2 159.3 %reduce-scatter.14.cloned.1.call-start = ((), (), s32[]{:S(2)}) async-start(), calls=%async_computation.14 | async-start | bytes 4718592 | tf_op jit(solution)/shard_map/reduce_scatter | solution.py:187
  691.6 7.8 copy-start.38
  709.2 178.3 %all-reduce.17.cloned.1.call-start = ((), (), s32[]{:S(2)}) async-start(), calls=%async_computation.16 | async-start | bytes 524288 | tf_op jit(solution)/shard_map/psum | solution.py:265
  710.9 3.9 copy-start.61
  714.7 40.3 %copy-start.18 = (bf16[788,512]{1,0:T(8,128)(2,1)S(1)}, bf16[788,512]{1,0:T(8,128)(2,1)}, u32[]{:S(2)}) copy-start(bf16[788,512]{1,0:T(8,128)(2,1)} %param.14) | copy-start | bytes 2420740
  714.7 40.3 %copy-start.23 = (f32[788,512]{1,0:T(8,128)S(1)}, f32[788,512]{1,0:T(8,128)}, u32[]{:S(2)}) copy-start(f32[788,512]{1,0:T(8,128)} %copy-done.21) | copy-start | bytes 4841476
  (30 other events, 56.0 us)
Sparse Core Ops, SparseCore 0:
  10.5 28.3 all-gather.4
  134.4 37.0 all-gather.6
  210.7 37.0 all-gather.8
  601.0 44.9 reduce-scatter.15
  653.3 45.4 reduce-scatter.9
  701.9 38.4 reduce-scatter.7
  743.8 51.0 reduce-scatter.11
  798.3 51.0 reduce-scatter.13
  851.8 35.6 all-reduce.16
